TPU v7x, 256 devices: a whole 4x4x8 slice. The times are simulated.
256 devices in a mesh: wide: 64 (over y, z, core), leaf: 4 (over x).
Axes of the slice: x: 4, y: 4, z: 8, core: 2. Of those that a mesh axis runs over, the one named last changes fastest.
Arguments:
- leaf_maps: float32 [64, 4, 2, 2, 512, 512], P('wide', 'leaf'), may hold values from -0.36 to 1.01
- angles: float32 [32], replicated, may hold values from -1.2 to 1.2
Outputs:
- reflected: float32 [64, 2, 64, 512], P('wide', None, 'leaf')
- transmitted: float32 [64, 2, 64, 512], P('wide', None, 'leaf')
All inputs are finite; a program needn't handle non-finite values.
Results may differ from a plain program's by a relative error of at most 0.0003.
Values sent between devices are 32-bit elements; how exact they have to be, the bound alone decides.
A program may use at most 320 MiB of HBM per device.

v0:
```python
import jax
import jax.numpy as jnp
from jax import lax
from jax.sharding import PartitionSpec as P

precise = lax.Precision.HIGHEST
wavenumber = 12.0


def from_partner(x, axis, apart):
    return lax.ppermute(x, axis, [(i, i ^ 1 << apart) for i in range(lax.axis_size(axis))])


def passed_along(x, axis, by):
    peers = lax.axis_size(axis)
    pairs = [(i, i + by) for i in range(peers) if 0 <= i + by < peers]
    return lax.ppermute(x, axis, pairs)


def plain_dot(left_mat, right_mat):
    return jnp.dot(left_mat, right_mat, precision=precise, preferred_element_type=jnp.float32)


def complex_dot(left_mat, right_mat):
    real_part = plain_dot(left_mat[0], right_mat[0]) - plain_dot(left_mat[1], right_mat[1])
    imag_part = plain_dot(left_mat[0], right_mat[1]) + plain_dot(left_mat[1], right_mat[0])
    return jnp.stack([real_part, imag_part])


def side_dot(vectors, matrix):
    return lax.dot_general(
        vectors,
        matrix,
        (((1,), (1,)), ((), ())),
        precision=precise,
        preferred_element_type=jnp.float32,
    )


def complex_apply(matrix, vectors):
    real_part = side_dot(vectors[0], matrix[0]) - side_dot(vectors[1], matrix[1])
    imag_part = side_dot(vectors[0], matrix[1]) + side_dot(vectors[1], matrix[0])
    return jnp.stack([real_part, imag_part])


def complex_solve(system, right_mat):
    size_n = system.shape[1]
    upper_band = jnp.concatenate([system[0], -system[1]], 1)
    lower_band = jnp.concatenate([system[1], system[0]], 1)
    big_mat = jnp.concatenate([upper_band, lower_band], 0)
    stacked = jnp.concatenate([right_mat[0], right_mat[1]], 0)
    normal = lax.dot_general(
        big_mat,
        big_mat,
        (((0,), (0,)), ((), ())),
        precision=precise,
        preferred_element_type=jnp.float32,
    )
    projected = lax.dot_general(
        big_mat,
        stacked,
        (((0,), (0,)), ((), ())),
        precision=precise,
        preferred_element_type=jnp.float32,
    )
    factor = jnp.linalg.cholesky(normal)
    solution = jax.scipy.linalg.cho_solve((factor, True), projected)
    return jnp.stack([solution[:size_n], solution[size_n:]])


def block_take(matrix, row_list, col_list):
    row_cat = jnp.concatenate([matrix[:, start_at:stop_at] for start_at, stop_at in row_list], 1)
    return jnp.concatenate([row_cat[:, :, start_at:stop_at] for start_at, stop_at in col_list], 2)


def merge_setup(map_lower, map_upper, side_pts, edge_pts, keeping):
    total_pts = 2 * side_pts + 2 * edge_pts
    lower_ext = 2 * side_pts + (edge_pts if keeping else 0)
    lower_outer = [(0, lower_ext)]
    lower_inner = [(2 * side_pts + edge_pts, total_pts)]
    upper_outer = [(0, 2 * side_pts)] + ([(2 * side_pts + edge_pts, total_pts)] if keeping else [])
    upper_inner = [(2 * side_pts, 2 * side_pts + edge_pts)]
    alpha_outer = block_take(map_lower, lower_outer, lower_outer)
    alpha_reach = block_take(map_lower, lower_outer, lower_inner)
    alpha_inward = block_take(map_lower, lower_inner, lower_outer)
    alpha_inner = block_take(map_lower, lower_inner, lower_inner)
    beta_outer = block_take(map_upper, upper_outer, upper_outer)
    beta_reach = block_take(map_upper, upper_outer, upper_inner)
    beta_inward = block_take(map_upper, upper_inner, upper_outer)
    beta_inner = block_take(map_upper, upper_inner, upper_inner)
    identity_mat = jnp.stack(
        [jnp.eye(edge_pts, dtype=jnp.float32), jnp.zeros((edge_pts, edge_pts), jnp.float32)]
    )
    system = identity_mat - complex_dot(beta_inner, alpha_inner)
    right_mat = jnp.concatenate([-complex_dot(beta_inner, alpha_inward), beta_inward], 2)
    solved = complex_solve(system, right_mat)
    blocks = (alpha_outer, alpha_reach, alpha_inward, alpha_inner, beta_outer, beta_reach)
    return (blocks, solved)


def rows_lower(blocks, solved):
    alpha_outer, alpha_reach = (blocks[0], blocks[1])
    upper_count = solved.shape[2] - alpha_outer.shape[2]
    padded = jnp.concatenate(
        [alpha_outer, jnp.zeros((2, alpha_outer.shape[1], upper_count), jnp.float32)], 2
    )
    return padded - complex_dot(alpha_reach, solved)


def rows_upper(blocks, solved):
    alpha_inward, alpha_inner, beta_outer, beta_reach = (blocks[2], blocks[3], blocks[4], blocks[5])
    leading = jnp.concatenate([-complex_dot(beta_reach, alpha_inward), beta_outer], 2)
    return leading + complex_dot(complex_dot(beta_reach, alpha_inner), solved)


def order_spans(side_pts, edge_pts, keeping):
    lower_ext = 2 * side_pts + (edge_pts if keeping else 0)
    starts = [
        (0, side_pts),
        (lower_ext, side_pts),
        (side_pts, side_pts),
        (lower_ext + side_pts, side_pts),
    ]
    if keeping:
        starts = starts + [(2 * side_pts, edge_pts), (lower_ext + 2 * side_pts, edge_pts)]
    return [(start_at, start_at + length) for start_at, length in starts]


def merge_boxes(map_lower, map_upper, side_pts, edge_pts, keeping):
    blocks, solved = merge_setup(map_lower, map_upper, side_pts, edge_pts, keeping)
    merged = jnp.concatenate([rows_lower(blocks, solved), rows_upper(blocks, solved)], 1)
    span_list = order_spans(side_pts, edge_pts, keeping)
    return block_take(merged, span_list, span_list)


def incident(position, thetas, face_pts, edge_pts):
    heights = (jnp.arange(face_pts, dtype=jnp.float32) + 0.5) / edge_pts
    across_x = jnp.cos(thetas)[:, None]
    along_y = jnp.sin(thetas)[:, None]
    left_phase = wavenumber * (position * across_x + heights[None, :] * along_y)
    right_phase = wavenumber * ((position + 1.0) * across_x + heights[None, :] * along_y)
    phases = jnp.concatenate([left_phase, right_phase], 1)
    return jnp.stack([jnp.cos(phases), jnp.sin(phases)])


def per_device(leaf_maps, angles):
    edge_pts = leaf_maps.shape[-1] // 4
    leaf_id = lax.axis_index("leaf")
    pol_id = leaf_id % 2
    half_id = leaf_id // 2
    own_maps = leaf_maps[0, 0]
    own_pol = lax.dynamic_index_in_dim(own_maps, pol_id, 0, keepdims=False)
    other_pol = lax.dynamic_index_in_dim(own_maps, 1 - pol_id, 0, keepdims=False)
    partner = from_partner(other_pol, "leaf", 0)
    is_lower = pol_id == 0
    paired = merge_boxes(
        jnp.where(is_lower, own_pol, partner),
        jnp.where(is_lower, partner, own_pol),
        edge_pts,
        edge_pts,
        True,
    )
    neighbor = from_partner(paired, "leaf", 1)
    lower_two = half_id == 0
    map_lower = jnp.where(lower_two, paired, neighbor)
    map_upper = jnp.where(lower_two, neighbor, paired)
    full_map = merge_boxes(map_lower, map_upper, 2 * edge_pts, edge_pts, False)
    face_pts = full_map.shape[1] // 2
    col_count = angles.shape[0] // 2
    thetas = lax.dynamic_slice_in_dim(angles, half_id * col_count, col_count)
    wide_id = lax.axis_index("wide")
    position = wide_id.astype(jnp.float32)
    incoming = incident(position, thetas, face_pts, edge_pts)
    driven = complex_apply(full_map, incoming)
    transfer = full_map[:, face_pts:, :face_pts]
    outgoing = driven[:, :, face_pts:]
    blank = jnp.zeros_like(outgoing)

    def advance(step_at, stored):
        sending = lax.cond(
            wide_id == step_at, lambda: outgoing + complex_apply(transfer, stored), lambda: blank
        )
        received = passed_along(sending, "wide", 1)
        return jnp.where(wide_id == step_at + 1, received, stored)

    chained = lax.fori_loop(0, lax.axis_size("wide") - 1, advance, blank)
    right_part = outgoing + complex_apply(transfer, chained)
    left_part = driven[:, :, :face_pts] + complex_apply(full_map[:, :face_pts, :face_pts], chained)
    return (left_part[None], right_part[None])


def solution(mesh):
    placed = (P("wide", "leaf", None, None, None, None), P())
    return jax.shard_map(
        per_device,
        mesh=mesh,
        in_specs=placed,
        out_specs=(P("wide", None, "leaf", None), P("wide", None, "leaf", None)),
        check_vma=False,
    )
```

profile of v0, /device:TPU:223, one launch (start us, length us, event | category | flops | bytes accessed | tf_op | source)
XLA Modules:
  0.0 914.9 jit_solution(14545849507933917135)
XLA Ops:
  3.6 45.5 %collective-permute-done.1 = f32[2,512,512]{2,1,0:T(8,128)} collective-permute-done((f32[2,512,512]{2,1,0:T(8,128)S(1)}, f32[2,512,512]{2,1,0:T(8,128)}, u32[]{:S(2)}, u32[]{:S(2)}) %collective-permute-start.1) | collective-permute-done | bytes 2097184 | tf_op jit(solution)/shard_map/ppermute | solution.py:11
  56.3 11.7 %cholesky.130 = f32[128,128]{1,0:T(8,128)S(1)} custom-call(f32[128,128]{1,0:T(8,128)S(1)} %cholesky.194), custom_call_target="Cholesky" | custom-call | tf_op jit(solution)/shard_map/jit(cholesky)/cholesky | solution.py:66
  68.1 9.8 %custom-call.26 = f32[1,128,128]{1,2,0:T(8,128)S(1)} custom-call(f32[1,128,128]{2,1,0:T(8,128)S(1)} %get-tuple-element.207), custom_call_target="InvertDiagBlocksLowerTriangular" | custom-call | tf_op jit(solution)/shard_map/jit(cholesky)/cholesky | solution.py:66
  80.0 11.9 %cholesky.147 = f32[128,128]{1,0:T(8,128)S(1)} custom-call(f32[128,128]{1,0:T(8,128)S(1)} %convolution_subtract_fusion.15), custom_call_target="Cholesky" | custom-call | tf_op jit(solution)/shard_map/jit(cholesky)/cholesky | solution.py:66
  99.2 19.7 %custom-call.22 = f32[2,128,128]{1,2,0:T(8,128)S(1)} custom-call(f32[2,128,128]{2,1,0:T(8,128)S(1)} %get-tuple-element.121), custom_call_target="InvertDiagBlocksLowerTriangular" | custom-call | tf_op jit(solution)/shard_map/jit(_cho_solve)/triangular_solve | solution.py:67
  133.4 12.3 %fusion.34 = f32[1,384,384]{2,1,0:T(8,128)S(1)} fusion(f32[384,384]{1,0:T(8,128)S(1)} %fusion.88, f32[384,128]{1,0:T(8,128)S(1)} %get-tuple-element.190, f32[2,512,512]{2,1,0:T(8,128)S(1)} %get-tuple-element.184), kind=kOutput, calls=%fused_computation.80 | convolution fusion | flops 226639872 | bytes 1572864 | tf_op jit(solution)/shard_map/dot_general | solution.py:21
  157.0 102.4 %collective-permute-done.2 = f32[2,768,768]{2,1,0:T(8,128)} collective-permute-done((f32[2,768,768]{2,1,0:T(8,128)}, f32[2,768,768]{2,1,0:T(8,128)}, u32[]{:S(2)}, u32[]{:S(2)}) %collective-permute-start.2) | collective-permute-done | bytes 4718624 | tf_op jit(solution)/shard_map/ppermute | solution.py:11
  280.2 13.2 %cholesky.164 = f32[128,128]{1,0:T(8,128)} custom-call(f32[128,128]{1,0:T(8,128)} %cholesky.197), custom_call_target="Cholesky" | custom-call | tf_op jit(solution)/shard_map/jit(cholesky)/cholesky | solution.py:66
  296.4 11.7 %custom-call.27 = f32[1,128,128]{1,2,0:T(8,128)} custom-call(f32[1,128,128]{2,1,0:T(8,128)} %get-tuple-element.203), custom_call_target="InvertDiagBlocksLowerTriangular" | custom-call | tf_op jit(solution)/shard_map/jit(cholesky)/cholesky | solution.py:66
  311.5 13.2 %cholesky.181 = f32[128,128]{1,0:T(8,128)} custom-call(f32[128,128]{1,0:T(8,128)} %convolution_subtract_fusion.13), custom_call_target="Cholesky" | custom-call | tf_op jit(solution)/shard_map/jit(cholesky)/cholesky | solution.py:66
  331.0 7.1 while.17
  338.1 21.1 %custom-call.23 = f32[2,128,128]{1,2,0:T(8,128)} custom-call(f32[2,128,128]{2,1,0:T(8,128)} %get-tuple-element.129), custom_call_target="InvertDiagBlocksLowerTriangular" | custom-call | tf_op jit(solution)/shard_map/jit(_cho_solve)/triangular_solve | solution.py:67
  409.3 494.4 %while.18 = (s32[]{:T(128)}, f32[2,16,512]{2,1,0:T(8,128)S(1)}, s32[]{:T(128)}, f32[2,512,512]{2,1,0:T(8,128)S(1)}, f32[2,16,512]{2,1,0:T(8,128)S(1)}, /*index=5*/s32[]{:T(128)}, s32[]{:T(128)}) while((s32[]{:T(128)}, f32[2,16,512]{2,1,0:T(8,128)S(1)}, s32[]{:T(128)}, f32[2,512,512]{2,1,0:T(8,128)S(1)}, ...), condition=%wide.region_7.9_spmd.clone, body=%wide.region_4.8_spmd.clone.sunk | while | flops 201424896 | bytes 5308600 | solution.py:186
  409.3 4.9 collective-permute-start
  507.9 4.9 collective-permute-done
  514.7 4.9 collective-permute-done
  521.6 4.9 collective-permute-done
  535.4 4.9 collective-permute-done
  542.3 4.9 collective-permute-done
  549.2 4.9 collective-permute-done
  556.1 4.9 collective-permute-done
  569.9 4.9 collective-permute-done
  576.8 4.9 collective-permute-done
  583.7 4.9 collective-permute-done
  590.6 4.9 collective-permute-done
  604.4 4.9 collective-permute-done
  611.3 4.9 collective-permute-done
  618.2 4.9 collective-permute-done
  638.8 4.9 collective-permute-done
  694.0 5.3 collective-permute-done
  701.3 5.8 collective-permute-done
  709.1 5.8 collective-permute-done
  716.9 5.8 collective-permute-done
  724.7 5.8 collective-permute-done
  732.4 5.8 collective-permute-done
  740.2 5.8 collective-permute-done
  748.0 5.8 collective-permute-done
  755.8 5.8 collective-permute-done
  763.6 5.8 collective-permute-done
  771.4 5.8 collective-permute-done
  779.2 5.8 collective-permute-done
  787.0 5.8 collective-permute-done
  794.8 5.8 collective-permute-done
  802.6 5.8 collective-permute-done
  810.4 5.8 collective-permute-done
  818.2 5.8 collective-permute-done
  826.0 60.8 %collective-permute-done = f32[2,16,512]{2,1,0:T(8,128)S(1)} collective-permute-done((f32[2,16,512]{2,1,0:T(8,128)S(1)}, f32[2,16,512]{2,1,0:T(8,128)S(1)}, u32[]{:S(2)}, u32[]{:S(2)}) %collective-permute-start) | collective-permute-done | bytes 65568 | tf_op jit(solution)/shard_map/while/body/eval_jaxpr/ppermute | solution.py:17
  894.1 8.2 collective-permute-start
  (572 shorter events, 398.1 us)
Async XLA Ops:
  2.4 46.7 %collective-permute-start.1 = (f32[2,512,512]{2,1,0:T(8,128)S(1)}, f32[2,512,512]{2,1,0:T(8,128)}, u32[]{:S(2)}, u32[]{:S(2)}) collective-permute-start(f32[2,512,512]{2,1,0:T(8,128)S(1)} %dynamic-slice_bitcast_fusion), channel_id=1, source_target_pairs={{0,1},{1,0},{2,3},{3,2},{4,5},{5,4},{6,7},{7,6},{8,9},{9,8},{10,11... | collective-permute-start | bytes 6291464 | tf_op jit(solution)/shard_map/ppermute | solution.py:11
  155.7 103.7 %collective-permute-start.2 = (f32[2,768,768]{2,1,0:T(8,128)}, f32[2,768,768]{2,1,0:T(8,128)}, u32[]{:S(2)}, u32[]{:S(2)}) collective-permute-start(f32[2,768,768]{2,1,0:T(8,128)} %slice_dynamic-update-slice_fusion), channel_id=1, source_target_pairs={{0,2},{1,3},{2,0},{3,1},{4,6},{5,7},{6,4},{7,5},{8,10},{9,11},{10,... | collective-permute-start | bytes 14155784 | tf_op jit(solution)/shard_map/ppermute | solution.py:11
  478.3 6.8 collective-permute-start
  485.2 6.8 collective-permute-start
  492.1 6.8 collective-permute-start
  499.0 6.8 collective-permute-start
  505.9 6.8 collective-permute-start
  512.8 6.8 collective-permute-start
  519.7 6.8 collective-permute-start
  526.6 6.8 collective-permute-start
  533.5 6.8 collective-permute-start
  540.4 6.8 collective-permute-start
  547.3 6.8 collective-permute-start
  554.2 6.8 collective-permute-start
  561.1 6.8 collective-permute-start
  568.0 6.8 collective-permute-start
  574.9 6.8 collective-permute-start
  581.7 6.8 collective-permute-start
  588.6 6.8 collective-permute-start
  595.5 6.8 collective-permute-start
  602.4 6.8 collective-permute-start
  609.3 6.8 collective-permute-start
  616.2 6.8 collective-permute-start
  623.1 6.8 collective-permute-start
  630.0 6.8 collective-permute-start
  636.9 6.8 collective-permute-start
  643.8 6.8 collective-permute-start
  650.7 6.8 collective-permute-start
  664.5 6.8 collective-permute-start
  692.0 7.2 collective-permute-start
  699.3 7.7 collective-permute-start
  707.1 7.7 collective-permute-start
  714.9 7.7 collective-permute-start
  722.7 7.7 collective-permute-start
  730.5 7.7 collective-permute-start
  738.3 7.7 collective-permute-start
  746.1 7.7 collective-permute-start
  753.9 7.7 collective-permute-start
  761.7 7.7 collective-permute-start
  769.5 7.7 collective-permute-start
  777.3 7.7 collective-permute-start
  785.1 7.7 collective-permute-start
  792.9 7.7 collective-permute-start
  800.6 7.7 collective-permute-start
  808.4 7.7 collective-permute-start
  816.2 7.7 collective-permute-start
  824.0 62.8 %collective-permute-start = (f32[2,16,512]{2,1,0:T(8,128)S(1)}, f32[2,16,512]{2,1,0:T(8,128)S(1)}, u32[]{:S(2)}, u32[]{:S(2)}) collective-permute-start(f32[2,16,512]{2,1,0:T(8,128)S(1)} %get-tuple-element.359), channel_id=1, source_target_pairs={{0,4},{4,8},{8,12},{12,16},{16,20},{20,24},{24,28},{28,32},{32,36}... | collective-permute-start | bytes 196616 | tf_op jit(solution)/shard_map/while/body/eval_jaxpr/ppermute | solution.py:17
  894.1 9.5 %collective-permute-start = (f32[2,16,512]{2,1,0:T(8,128)S(1)}, f32[2,16,512]{2,1,0:T(8,128)S(1)}, u32[]{:S(2)}, u32[]{:S(2)}) collective-permute-start(f32[2,16,512]{2,1,0:T(8,128)S(1)} %get-tuple-element.359), channel_id=1, source_target_pairs={{0,4},{4,8},{8,12},{12,16},{16,20},{20,24},{24,28},{28,32},{32,36}... | collective-permute-start | bytes 196616 | tf_op jit(solution)/shard_map/while/body/eval_jaxpr/ppermute | solution.py:17
  (43 other events, 250.1 us)
where the time goes:
time: 933 us; the launch traced here: 915 us
  waiting for transfers between devices  472 us (51%)
  starting transfers between devices  161 us (17%)
  other arithmetic  140 us (15%)
  matrix products  100 us (11%)
  local copies, waits for them, and re-layouts  31.8 us (3%)
    ppermute x63, waiting for transfers between devices, passed_along(): return lax.ppermute(x, axis, pairs)  324 us
    ppermute x63, starting transfers between devices, passed_along(): return lax.ppermute(x, axis, pairs)  159 us
    ppermute x2, waiting for transfers between devices, from_partner(): lax.ppermute(x, axis, [(i, i ^ 1 << apart) for i in range(lax.axis_size(a...  148 us
    another operation x13, other arithmetic, complex_solve(): factor = jnp.linalg.cholesky(normal)  76.5 us
    dot_general x48, matrix products, plain_dot(): jnp.dot(left_mat, right_mat, precision=precise, preferred_element_type=jn...  55.7 us
    another operation x5, other arithmetic, complex_solve(): solution = jax.scipy.linalg.cho_solve((factor, True), projected)  43 us
    dot_general x16, matrix products, side_dot(): lax.dot_general(vectors, matrix, (((1,), (1,)), ((), ())), precision=prec...  28.1 us
  transfers between devices with their start and end apart: 65, of which 65 were waited for; matrix products, arithmetic and copies ran while one was open for 0% of the time, Pallas kernels for 0%

commit v1 on v0

--- a/solution.py
+++ b/solution.py
@@ -143,6 +143,31 @@
     return jnp.stack([jnp.cos(phases), jnp.sin(phases)])
 
 
+def shifted_along(x, axis, pairs):
+    return lax.ppermute(x, axis, pairs)
+
+
+def trim_pair(paired, lower_two, side_pts, edge_pts):
+    kept_lower = [(0, 2 * side_pts), (2 * side_pts + edge_pts, 2 * side_pts + 2 * edge_pts)]
+    kept_upper = [(0, 2 * side_pts + edge_pts)]
+    return jnp.where(
+        lower_two,
+        block_take(paired, kept_lower, kept_lower),
+        block_take(paired, kept_upper, kept_upper),
+    )
+
+
+def untrim_pair(small, from_lower, side_pts, edge_pts):
+    lead = 2 * side_pts
+    zero_col = jnp.zeros((2, small.shape[1], edge_pts), jnp.float32)
+    zero_row = jnp.zeros((2, edge_pts, small.shape[2] + edge_pts), jnp.float32)
+    as_lower = jnp.concatenate([small[:, :, :lead], zero_col, small[:, :, lead:]], 2)
+    as_lower = jnp.concatenate([as_lower[:, :lead], zero_row, as_lower[:, lead:]], 1)
+    as_upper = jnp.concatenate([small, zero_col], 2)
+    as_upper = jnp.concatenate([as_upper, zero_row], 1)
+    return jnp.where(from_lower, as_lower, as_upper)
+
+
 def per_device(leaf_maps, angles):
     edge_pts = leaf_maps.shape[-1] // 4
     leaf_id = lax.axis_index("leaf")
@@ -160,8 +185,9 @@
         edge_pts,
         True,
     )
-    neighbor = from_partner(paired, "leaf", 1)
     lower_two = half_id == 0
+    sent_pair = trim_pair(paired, lower_two, 2 * edge_pts, edge_pts)
+    neighbor = untrim_pair(from_partner(sent_pair, "leaf", 1), jnp.logical_not(lower_two), 2 * edge_pts, edge_pts)
     map_lower = jnp.where(lower_two, paired, neighbor)
     map_upper = jnp.where(lower_two, neighbor, paired)
     full_map = merge_boxes(map_lower, map_upper, 2 * edge_pts, edge_pts, False)
@@ -169,6 +195,7 @@
     col_count = angles.shape[0] // 2
     thetas = lax.dynamic_slice_in_dim(angles, half_id * col_count, col_count)
     wide_id = lax.axis_index("wide")
+    wide_count = lax.axis_size("wide")
     position = wide_id.astype(jnp.float32)
     incoming = incident(position, thetas, face_pts, edge_pts)
     driven = complex_apply(full_map, incoming)
@@ -176,14 +203,29 @@
     outgoing = driven[:, :, face_pts:]
     blank = jnp.zeros_like(outgoing)
 
+    to_odd = [(i, i + 1) for i in range(0, wide_count, 2)]
+    handed = shifted_along(jnp.concatenate([transfer, outgoing], 1), "wide", to_odd)
+    prev_transfer = handed[:, :face_pts]
+    prev_outgoing = handed[:, face_pts:]
+    double_map = complex_dot(transfer, prev_transfer)
+    double_drive = outgoing + complex_apply(transfer, prev_outgoing)
+
+    odd_pairs = [(i, i + 2) for i in range(1, wide_count - 2, 2)]
+
     def advance(step_at, stored):
+        active = wide_id == 2 * step_at + 1
         sending = lax.cond(
-            wide_id == step_at, lambda: outgoing + complex_apply(transfer, stored), lambda: blank
+            active, lambda: double_drive + complex_apply(double_map, stored), lambda: blank
         )
-        received = passed_along(sending, "wide", 1)
-        return jnp.where(wide_id == step_at + 1, received, stored)
-
-    chained = lax.fori_loop(0, lax.axis_size("wide") - 1, advance, blank)
+        received = shifted_along(sending, "wide", odd_pairs)
+        return jnp.where(wide_id == 2 * step_at + 3, received, stored)
+
+    even_in = lax.fori_loop(0, wide_count // 2 - 1, advance, blank)
+    to_even = [(i + 1, i) for i in range(0, wide_count, 2)]
+    given = shifted_along(even_in, "wide", to_even)
+    is_odd = wide_id % 2 == 1
+    odd_in = prev_outgoing + complex_apply(prev_transfer, even_in)
+    chained = jnp.where(is_odd, odd_in, given)
     right_part = outgoing + complex_apply(transfer, chained)
     left_part = driven[:, :, :face_pts] + complex_apply(full_map[:, :face_pts, :face_pts], chained)
     return (left_part[None], right_part[None])

time: 933 us -> 703 us (0.75)
  waiting for transfers between devices: 472 us -> 308 us
  starting transfers between devices: 161 us -> 66.7 us
  other arithmetic: 140 us -> 158 us
  matrix products: 100 us -> 114 us
    ppermute x63 -> x33, waiting for transfers between devices: 324 us -> 191 us  [shifted_along(): return lax.ppermute(x, axis, pairs)]
    ppermute x63 -> x33, starting transfers between devices: 159 us -> 65 us  [shifted_along(): return lax.ppermute(x, axis, pairs)]
    ppermute x2, waiting for transfers between devices: 148 us -> 117 us  [from_partner(): lax.ppermute(x, axis, [(i, i ^ 1 << apart) for i in range(lax.axis_size(a...]
    dot_general x16 -> x24, matrix products: 28.1 us -> 42.5 us  [side_dot(): lax.dot_general(vectors, matrix, (((1,), (1,)), ((), ())), precision=prec...]
    another operation x13, other arithmetic: 76.5 us -> 89.1 us  [complex_solve(): factor = jnp.linalg.cholesky(normal)]
    dot_general x48 -> x52, matrix products: 55.7 us -> 57.9 us  [plain_dot(): jnp.dot(left_mat, right_mat, precision=precise, preferred_element_type=jn...]
  transfers between devices with their start and end apart: 65 -> 35, of which waited for: 65 -> 34; matrix products, arithmetic and copies ran while one was open for 0% -> 2% of each run, Pallas kernels for 0% -> 0%
where the time goes in v1:
time: 703 us; the launch traced here: 692 us
  waiting for transfers between devices  308 us (44%)
  other arithmetic  158 us (22%)
  matrix products  114 us (16%)
  starting transfers between devices  66.7 us (9%)
  local copies, waits for them, and re-layouts  36.8 us (5%)
    ppermute x33, waiting for transfers between devices, shifted_along(): return lax.ppermute(x, axis, pairs)  191 us
    ppermute x2, waiting for transfers between devices, from_partner(): lax.ppermute(x, axis, [(i, i ^ 1 << apart) for i in range(lax.axis_size(a...  117 us
    another operation x13, other arithmetic, complex_solve(): factor = jnp.linalg.cholesky(normal)  89.1 us
    ppermute x33, starting transfers between devices, shifted_along(): return lax.ppermute(x, axis, pairs)  65 us
    dot_general x52, matrix products, plain_dot(): jnp.dot(left_mat, right_mat, precision=precise, preferred_element_type=jn...  57.9 us
    another operation x5, other arithmetic, complex_solve(): solution = jax.scipy.linalg.cho_solve((factor, True), projected)  43.2 us
    dot_general x24, matrix products, side_dot(): lax.dot_general(vectors, matrix, (((1,), (1,)), ((), ())), precision=prec...  42.5 us
  transfers between devices with their start and end apart: 35, of which 34 were waited for; matrix products, arithmetic and copies ran while one was open for 2% of the time, Pallas kernels for 0%

profile of v1, /device:TPU:223, one launch (start us, length us, event | category | flops | bytes accessed | tf_op | source)
XLA Modules:
  0.0 691.9 jit_solution(664700279548758761)
XLA Ops:
  3.6 45.6 %collective-permute-done.1 = f32[2,512,512]{2,1,0:T(8,128)} collective-permute-done((f32[2,512,512]{2,1,0:T(8,128)S(1)}, f32[2,512,512]{2,1,0:T(8,128)}, u32[]{:S(2)}, u32[]{:S(2)}) %collective-permute-start.1) | collective-permute-done | bytes 2097184 | tf_op jit(solution)/shard_map/ppermute | solution.py:11
  67.6 13.2 %cholesky.130 = f32[128,128]{1,0:T(8,128)} custom-call(f32[128,128]{1,0:T(8,128)} %cholesky.194), custom_call_target="Cholesky" | custom-call | tf_op jit(solution)/shard_map/jit(cholesky)/cholesky | solution.py:66
  84.4 11.3 %custom-call.26 = f32[1,128,128]{1,2,0:T(8,128)} custom-call(f32[1,128,128]{2,1,0:T(8,128)} %get-tuple-element.243), custom_call_target="InvertDiagBlocksLowerTriangular" | custom-call | tf_op jit(solution)/shard_map/jit(cholesky)/cholesky | solution.py:66
  99.1 25.0 %cholesky.147 = f32[128,128]{1,0:T(8,128)} custom-call(f32[128,128]{1,0:T(8,128)} %convolution_subtract_fusion.16), custom_call_target="Cholesky" | custom-call | tf_op jit(solution)/shard_map/jit(cholesky)/cholesky | solution.py:66
  131.8 8.2 %while.16 = (s32[]{:T(128)}, f32[256,256]{1,0:T(8,128)}, s32[2,2]{1,0:T(2,128)}, f32[2,128,128]{2,1,0:T(8,128)}, s32[]{:T(128)}) while((s32[]{:T(128)}, f32[256,256]{1,0:T(8,128)}, s32[2,2]{1,0:T(2,128)}, f32[2,128,128]{2,1,0:T(8,128)}, s32[]{:T(128)}) %tuple.106), condition=%wide.while_cond, body=%wide.while_body.sunk | while | flops 2 | bytes 132705 | solution.py:67
  140.0 21.1 %custom-call.22 = f32[2,128,128]{1,2,0:T(8,128)} custom-call(f32[2,128,128]{2,1,0:T(8,128)} %get-tuple-element.139), custom_call_target="InvertDiagBlocksLowerTriangular" | custom-call | tf_op jit(solution)/shard_map/jit(_cho_solve)/triangular_solve | solution.py:67
  189.0 71.3 %collective-permute-done.2 = f32[2,640,640]{2,1,0:T(8,128)S(1)} collective-permute-done((f32[2,640,640]{2,1,0:T(8,128)}, f32[2,640,640]{2,1,0:T(8,128)S(1)}, u32[]{:S(2)}, u32[]{:S(2)}) %collective-permute-start.2) | collective-permute-done | bytes 3276832 | tf_op jit(solution)/shard_map/ppermute | solution.py:11
  270.4 11.7 %cholesky.164 = f32[128,128]{1,0:T(8,128)S(1)} custom-call(f32[128,128]{1,0:T(8,128)S(1)} %cholesky.197), custom_call_target="Cholesky" | custom-call | tf_op jit(solution)/shard_map/jit(cholesky)/cholesky | solution.py:66
  282.2 9.8 %custom-call.27 = f32[1,128,128]{1,2,0:T(8,128)S(1)} custom-call(f32[1,128,128]{2,1,0:T(8,128)S(1)} %get-tuple-element.239), custom_call_target="InvertDiagBlocksLowerTriangular" | custom-call | tf_op jit(solution)/shard_map/jit(cholesky)/cholesky | solution.py:66
  292.5 11.7 %cholesky.181 = f32[128,128]{1,0:T(8,128)S(1)} custom-call(f32[128,128]{1,0:T(8,128)S(1)} %convolution_subtract_fusion.14), custom_call_target="Cholesky" | custom-call | tf_op jit(solution)/shard_map/jit(cholesky)/cholesky | solution.py:66
  307.2 4.0 while.17
  311.2 19.7 %custom-call.23 = f32[2,128,128]{1,2,0:T(8,128)S(1)} custom-call(f32[2,128,128]{2,1,0:T(8,128)S(1)} %get-tuple-element.147), custom_call_target="InvertDiagBlocksLowerTriangular" | custom-call | tf_op jit(solution)/shard_map/jit(_cho_solve)/triangular_solve | solution.py:67
  369.9 3.7 fusion.12
  373.6 3.7 fusion.13
  377.3 3.7 fusion.36
  381.0 3.9 fusion.34
  390.5 3.7 collective-permute-done.3
  407.4 3.1 convolution_add_fusion.3
  413.5 257.6 %while.18 = (s32[]{:T(128)}, f32[2,16,512]{2,1,0:T(8,128)S(1)}, s32[]{:T(128)}, f32[512,512]{1,0:T(8,128)S(1)}, f32[512,512]{1,0:T(8,128)S(1)}, /*index=5*/f32[2...) while((s32[]{:T(128)}, f32[2,16,512]{2,1,0:T(8,128)S(1)}, s32[]{:T(128)}, ...), condition=%wide.region_7.9_spmd.clone, body=%wide.region_4.8_spmd.clone.sunk | while | flops 201424896 | bytes 5308668 | solution.py:223
  431.8 3.3 collective-permute-done
  437.2 4.3 collective-permute-done
  443.5 4.3 collective-permute-done
  449.8 4.3 collective-permute-done
  456.2 4.3 collective-permute-done
  462.5 4.3 collective-permute-done
  468.8 4.3 collective-permute-done
  475.1 4.3 collective-permute-done
  481.4 4.3 collective-permute-done
  487.8 4.3 collective-permute-done
  494.1 4.3 collective-permute-done
  500.4 4.3 collective-permute-done
  506.7 4.3 collective-permute-done
  513.0 5.0 collective-permute-done
  520.1 5.2 collective-permute-done
  527.3 5.2 collective-permute-done
  534.5 5.2 collective-permute-done
  541.8 5.2 collective-permute-done
  549.0 5.2 collective-permute-done
  556.2 5.2 collective-permute-done
  563.4 5.2 collective-permute-done
  570.6 5.2 collective-permute-done
  577.9 5.2 collective-permute-done
  585.1 5.2 collective-permute-done
  592.3 5.2 collective-permute-done
  599.5 5.2 collective-permute-done
  606.7 55.3 %collective-permute-done = f32[2,16,512]{2,1,0:T(8,128)S(1)} collective-permute-done((f32[2,16,512]{2,1,0:T(8,128)S(1)}, f32[2,16,512]{2,1,0:T(8,128)S(1)}, u32[]{:S(2)}, u32[]{:S(2)}) %collective-permute-start) | collective-permute-done | bytes 65568 | tf_op jit(solution)/shard_map/while/body/eval_jaxpr/ppermute | solution.py:147
  662.1 3.9 conditional.3
  668.0 3.1 collective-permute-done
  (430 shorter events, 242.1 us)
Async XLA Ops:
  2.4 46.7 %collective-permute-start.1 = (f32[2,512,512]{2,1,0:T(8,128)S(1)}, f32[2,512,512]{2,1,0:T(8,128)}, u32[]{:S(2)}, u32[]{:S(2)}) collective-permute-start(f32[2,512,512]{2,1,0:T(8,128)S(1)} %dynamic-slice_bitcast_fusion), channel_id=1, source_target_pairs={{0,1},{1,0},{2,3},{3,2},{4,5},{5,4},{6,7},{7,6},{8,9},{9,8},{10,11... | collective-permute-start | bytes 6291464 | tf_op jit(solution)/shard_map/ppermute | solution.py:11
  52.2 4.1 copy-start.9
  52.3 8.9 %copy-start.11 = (f32[2,128,512]{2,1,0:T(8,128)}, f32[2,128,512]{2,1,0:T(8,128)S(1)}, u32[]{:S(2)}) copy-start(f32[2,128,512]{2,1,0:T(8,128)S(1)} %slice.636) | copy-start | bytes 1572868
  53.6 8.7 %copy-start.23 = (f32[128,128]{0,1:T(8,128)}, f32[128,128]{0,1:T(8,128)S(1)}, u32[]{:S(2)}) copy-start(f32[128,128]{0,1:T(8,128)S(1)} %get-tuple-element.234) | copy-start | bytes 196612
  53.6 8.6 %copy-start.25 = (f32[128,128]{0,1:T(8,128)}, f32[128,128]{0,1:T(8,128)S(1)}, u32[]{:S(2)}) copy-start(f32[128,128]{0,1:T(8,128)S(1)} %get-tuple-element.235) | copy-start | bytes 196612
  53.6 8.6 %copy-start.21 = (f32[128,128]{0,1:T(8,128)}, f32[128,128]{0,1:T(8,128)S(1)}, u32[]{:S(2)}) copy-start(f32[128,128]{0,1:T(8,128)S(1)} %fusion.151) | copy-start | bytes 196612
  187.6 72.7 %collective-permute-start.2 = (f32[2,640,640]{2,1,0:T(8,128)}, f32[2,640,640]{2,1,0:T(8,128)S(1)}, u32[]{:S(2)}, u32[]{:S(2)}) collective-permute-start(f32[2,640,640]{2,1,0:T(8,128)} %slice_select_fusion), channel_id=1, source_target_pairs={{0,2},{1,3},{2,0},{3,1},{4,6},{5,7},{6,4},{7,5},{8,10},{9,11},{10,... | collective-permute-start | bytes 9830408 | tf_op jit(solution)/shard_map/ppermute | solution.py:11
  269.7 37.4 %copy-start.28 = (s32[2,2]{1,0:T(2,128)S(1)}, s32[2,2]{1,0:T(2,128)}, u32[]{:S(2)}) copy-start(s32[2,2]{1,0:T(2,128)} %get-tuple-element.419) | copy-start | bytes 52
  282.2 55.1 %slice-start = ((s8[4718592]{0:T(1024)(128)(4,1)}), s8[524288]{0:T(1024)(128)(4,1)S(1)}, s32[]{:S(2)}) async-start(s8[4718592]{0:T(1024)(128)(4,1)} %bitcast.397), calls=%async_computation | async-start | bytes 1048576
  335.4 4.6 slice-start.2
  367.1 20.7 %copy-start = (f32[2,1024,256]{2,1,0:T(8,128)}, f32[2,1024,256]{2,1,0:T(8,128)S(1)}, u32[]{:S(2)}) copy-start(f32[2,1024,256]{2,1,0:T(8,128)S(1)} %get-tuple-element.203) | copy-start | bytes 6291460
  386.5 7.7 %collective-permute-start.3 = (f32[2,528,512]{2,1,0:T(8,128)}, f32[2,528,512]{2,1,0:T(8,128)}, u32[]{:S(2)}, u32[]{:S(2)}) collective-permute-start(f32[2,528,512]{2,1,0:T(8,128)} %pad_maximum_fusion.3), channel_id=1, source_target_pairs={{0,4},{8,12},{16,20},{24,28},{32,36},{40,44},{48,52},{56,60},{64,6... | collective-permute-start | bytes 6488072 | tf_op jit(solution)/shard_map/ppermute | solution.py:147
  390.5 19.9 %copy-start.4 = (f32[512,512]{1,0:T(8,128)}, f32[512,512]{1,0:T(8,128)S(1)}, u32[]{:S(2)}) copy-start(f32[512,512]{1,0:T(8,128)S(1)} %get-tuple-element.220) | copy-start | bytes 3145732
  413.8 5.0 collective-permute-start
  419.0 5.0 collective-permute-start
  424.1 5.0 collective-permute-start
  429.2 6.0 collective-permute-start
  435.2 6.2 collective-permute-start
  441.6 6.2 collective-permute-start
  447.9 6.2 collective-permute-start
  454.2 6.2 collective-permute-start
  460.5 6.2 collective-permute-start
  466.9 6.2 collective-permute-start
  473.2 6.2 collective-permute-start
  479.5 6.2 collective-permute-start
  485.8 6.2 collective-permute-start
  492.1 6.2 collective-permute-start
  498.5 6.2 collective-permute-start
  504.8 6.2 collective-permute-start
  511.1 7.0 %collective-permute-start = (f32[2,16,512]{2,1,0:T(8,128)S(1)}, f32[2,16,512]{2,1,0:T(8,128)S(1)}, u32[]{:S(2)}, u32[]{:S(2)}) collective-permute-start(f32[2,16,512]{2,1,0:T(8,128)S(1)} %get-tuple-element.410), channel_id=1, source_target_pairs={{4,12},{12,20},{20,28},{28,36},{36,44},{44,52},{52,60},{60,68},{68... | collective-permute-start | bytes 196616 | tf_op jit(solution)/shard_map/while/body/eval_jaxpr/ppermute | solution.py:147
  518.2 7.1 %collective-permute-start = (f32[2,16,512]{2,1,0:T(8,128)S(1)}, f32[2,16,512]{2,1,0:T(8,128)S(1)}, u32[]{:S(2)}, u32[]{:S(2)}) collective-permute-start(f32[2,16,512]{2,1,0:T(8,128)S(1)} %get-tuple-element.410), channel_id=1, source_target_pairs={{4,12},{12,20},{20,28},{28,36},{36,44},{44,52},{52,60},{60,68},{68... | collective-permute-start | bytes 196616 | tf_op jit(solution)/shard_map/while/body/eval_jaxpr/ppermute | solution.py:147
  525.4 7.1 %collective-permute-start = (f32[2,16,512]{2,1,0:T(8,128)S(1)}, f32[2,16,512]{2,1,0:T(8,128)S(1)}, u32[]{:S(2)}, u32[]{:S(2)}) collective-permute-start(f32[2,16,512]{2,1,0:T(8,128)S(1)} %get-tuple-element.410), channel_id=1, source_target_pairs={{4,12},{12,20},{20,28},{28,36},{36,44},{44,52},{52,60},{60,68},{68... | collective-permute-start | bytes 196616 | tf_op jit(solution)/shard_map/while/body/eval_jaxpr/ppermute | solution.py:147
  532.6 7.1 %collective-permute-start = (f32[2,16,512]{2,1,0:T(8,128)S(1)}, f32[2,16,512]{2,1,0:T(8,128)S(1)}, u32[]{:S(2)}, u32[]{:S(2)}) collective-permute-start(f32[2,16,512]{2,1,0:T(8,128)S(1)} %get-tuple-element.410), channel_id=1, source_target_pairs={{4,12},{12,20},{20,28},{28,36},{36,44},{44,52},{52,60},{60,68},{68... | collective-permute-start | bytes 196616 | tf_op jit(solution)/shard_map/while/body/eval_jaxpr/ppermute | solution.py:147
  539.8 7.1 %collective-permute-start = (f32[2,16,512]{2,1,0:T(8,128)S(1)}, f32[2,16,512]{2,1,0:T(8,128)S(1)}, u32[]{:S(2)}, u32[]{:S(2)}) collective-permute-start(f32[2,16,512]{2,1,0:T(8,128)S(1)} %get-tuple-element.410), channel_id=1, source_target_pairs={{4,12},{12,20},{20,28},{28,36},{36,44},{44,52},{52,60},{60,68},{68... | collective-permute-start | bytes 196616 | tf_op jit(solution)/shard_map/while/body/eval_jaxpr/ppermute | solution.py:147
  547.0 7.1 %collective-permute-start = (f32[2,16,512]{2,1,0:T(8,128)S(1)}, f32[2,16,512]{2,1,0:T(8,128)S(1)}, u32[]{:S(2)}, u32[]{:S(2)}) collective-permute-start(f32[2,16,512]{2,1,0:T(8,128)S(1)} %get-tuple-element.410), channel_id=1, source_target_pairs={{4,12},{12,20},{20,28},{28,36},{36,44},{44,52},{52,60},{60,68},{68... | collective-permute-start | bytes 196616 | tf_op jit(solution)/shard_map/while/body/eval_jaxpr/ppermute | solution.py:147
  554.3 7.1 %collective-permute-start = (f32[2,16,512]{2,1,0:T(8,128)S(1)}, f32[2,16,512]{2,1,0:T(8,128)S(1)}, u32[]{:S(2)}, u32[]{:S(2)}) collective-permute-start(f32[2,16,512]{2,1,0:T(8,128)S(1)} %get-tuple-element.410), channel_id=1, source_target_pairs={{4,12},{12,20},{20,28},{28,36},{36,44},{44,52},{52,60},{60,68},{68... | collective-permute-start | bytes 196616 | tf_op jit(solution)/shard_map/while/body/eval_jaxpr/ppermute | solution.py:147
  561.5 7.1 %collective-permute-start = (f32[2,16,512]{2,1,0:T(8,128)S(1)}, f32[2,16,512]{2,1,0:T(8,128)S(1)}, u32[]{:S(2)}, u32[]{:S(2)}) collective-permute-start(f32[2,16,512]{2,1,0:T(8,128)S(1)} %get-tuple-element.410), channel_id=1, source_target_pairs={{4,12},{12,20},{20,28},{28,36},{36,44},{44,52},{52,60},{60,68},{68... | collective-permute-start | bytes 196616 | tf_op jit(solution)/shard_map/while/body/eval_jaxpr/ppermute | solution.py:147
  568.7 7.1 %collective-permute-start = (f32[2,16,512]{2,1,0:T(8,128)S(1)}, f32[2,16,512]{2,1,0:T(8,128)S(1)}, u32[]{:S(2)}, u32[]{:S(2)}) collective-permute-start(f32[2,16,512]{2,1,0:T(8,128)S(1)} %get-tuple-element.410), channel_id=1, source_target_pairs={{4,12},{12,20},{20,28},{28,36},{36,44},{44,52},{52,60},{60,68},{68... | collective-permute-start | bytes 196616 | tf_op jit(solution)/shard_map/while/body/eval_jaxpr/ppermute | solution.py:147
  575.9 7.1 %collective-permute-start = (f32[2,16,512]{2,1,0:T(8,128)S(1)}, f32[2,16,512]{2,1,0:T(8,128)S(1)}, u32[]{:S(2)}, u32[]{:S(2)}) collective-permute-start(f32[2,16,512]{2,1,0:T(8,128)S(1)} %get-tuple-element.410), channel_id=1, source_target_pairs={{4,12},{12,20},{20,28},{28,36},{36,44},{44,52},{52,60},{60,68},{68... | collective-permute-start | bytes 196616 | tf_op jit(solution)/shard_map/while/body/eval_jaxpr/ppermute | solution.py:147
  583.1 7.1 %collective-permute-start = (f32[2,16,512]{2,1,0:T(8,128)S(1)}, f32[2,16,512]{2,1,0:T(8,128)S(1)}, u32[]{:S(2)}, u32[]{:S(2)}) collective-permute-start(f32[2,16,512]{2,1,0:T(8,128)S(1)} %get-tuple-element.410), channel_id=1, source_target_pairs={{4,12},{12,20},{20,28},{28,36},{36,44},{44,52},{52,60},{60,68},{68... | collective-permute-start | bytes 196616 | tf_op jit(solution)/shard_map/while/body/eval_jaxpr/ppermute | solution.py:147
  590.4 7.1 %collective-permute-start = (f32[2,16,512]{2,1,0:T(8,128)S(1)}, f32[2,16,512]{2,1,0:T(8,128)S(1)}, u32[]{:S(2)}, u32[]{:S(2)}) collective-permute-start(f32[2,16,512]{2,1,0:T(8,128)S(1)} %get-tuple-element.410), channel_id=1, source_target_pairs={{4,12},{12,20},{20,28},{28,36},{36,44},{44,52},{52,60},{60,68},{68... | collective-permute-start | bytes 196616 | tf_op jit(solution)/shard_map/while/body/eval_jaxpr/ppermute | solution.py:147
  597.6 7.1 %collective-permute-start = (f32[2,16,512]{2,1,0:T(8,128)S(1)}, f32[2,16,512]{2,1,0:T(8,128)S(1)}, u32[]{:S(2)}, u32[]{:S(2)}) collective-permute-start(f32[2,16,512]{2,1,0:T(8,128)S(1)} %get-tuple-element.410), channel_id=1, source_target_pairs={{4,12},{12,20},{20,28},{28,36},{36,44},{44,52},{52,60},{60,68},{68... | collective-permute-start | bytes 196616 | tf_op jit(solution)/shard_map/while/body/eval_jaxpr/ppermute | solution.py:147
  604.8 57.2 %collective-permute-start = (f32[2,16,512]{2,1,0:T(8,128)S(1)}, f32[2,16,512]{2,1,0:T(8,128)S(1)}, u32[]{:S(2)}, u32[]{:S(2)}) collective-permute-start(f32[2,16,512]{2,1,0:T(8,128)S(1)} %get-tuple-element.410), channel_id=1, source_target_pairs={{4,12},{12,20},{20,28},{28,36},{36,44},{44,52},{52,60},{60,68},{68... | collective-permute-start | bytes 196616 | tf_op jit(solution)/shard_map/while/body/eval_jaxpr/ppermute | solution.py:147
  666.1 5.0 collective-permute-start
  671.1 10.3 %collective-permute-start.4 = (f32[2,16,512]{2,1,0:T(8,128)S(1)}, f32[2,16,512]{2,1,0:T(8,128)S(1)}, u32[]{:S(2)}, u32[]{:S(2)}) collective-permute-start(f32[2,16,512]{2,1,0:T(8,128)S(1)} %get-tuple-element.131), channel_id=1, source_target_pairs={{4,0},{12,8},{20,16},{28,24},{36,32},{44,40},{52,48},{60,56},{68,6... | collective-permute-start | bytes 196616 | tf_op jit(solution)/shard_map/ppermute | solution.py:147
  674.6 8.7 %copy-start.5 = (f32[512,512]{1,0:T(8,128)S(1)}, f32[512,512]{1,0:T(8,128)}, u32[]{:S(2)}) copy-start(f32[512,512]{1,0:T(8,128)} %copy-done.4) | copy-start | bytes 3145732
  676.9 7.4 %copy-start.1 = (f32[2,1024,256]{2,1,0:T(8,128)S(1)}, f32[2,1024,256]{2,1,0:T(8,128)}, u32[]{:S(2)}) copy-start(f32[2,1024,256]{2,1,0:T(8,128)} %copy-done) | copy-start | bytes 6291460
  676.9 7.4 %copy-start.3 = (f32[2,1024,256]{2,1,0:T(8,128)S(1)}, f32[2,1024,256]{2,1,0:T(8,128)}, u32[]{:S(2)}) copy-start(f32[2,1024,256]{2,1,0:T(8,128)} %copy-done.2) | copy-start | bytes 6291460
  (22 other events, 48.7 us)
